TPU v7x, 32 devices: a whole 2x2x4 slice. The times are simulated.
32 devices in a mesh: boson: 8 (over z, x), block: 4 (over y, core).
Axes of the slice: x: 2, y: 2, z: 4, core: 2. Of those that a mesh axis runs over, the one named last changes fastest.
Arguments:
- gamma_ph: bfloat16 [32, 1024, 1024], P('boson', 'block'), may hold values from -6 to 6
- full_ph: bfloat16 [32, 1024, 1024], P('boson', 'block'), may hold values from -0.1875 to 0.1875
- chi_ph: float32 [32, 1024], P('boson'), may hold values from 0.3 to 3
- pp_vertex: bfloat16 [32, 1024, 1024], P('boson', 'block'), may hold values from -0.1875 to 0.1875
- chi_pp: float32 [32, 1024], P('boson'), may hold values from 0.3 to 3
- relabel: int32 [32, 16, 8], replicated, may hold values from 0 to 31, as said below
Outputs:
- vertex_new: bfloat16 [32, 1024, 1024], P('boson', 'block')
Inputs may be any that keep to these rules, and one draw needn't show every extreme that they name: `relabel`: for each row tile and column block the table is a permutation of the 32 points. The owner of the target point (target // 4) is the source's owner (q // 4) plus a shift modulo 8, and both this shift and the target's position among its owner's points (target % 4) depend only on the row tile, the column block and q % 4. Row tiles b * 4 to (b + 1) * 4 - 1 form row block b; within one row block, at most 17 of the 128 triples of position, row tile and column block share a shift, and some shift is shared by exactly 17; in every row block the shifts 1, 4 and 7 each occur.
All inputs are finite; a program needn't handle non-finite values.
Results may differ from a plain program's by a relative error of at most 0.0063.
Values may be sent and summed in bfloat16 or wider, within the bound.
A program may use at most 128 MiB of HBM per device.

v0:
```python
import jax
import jax.numpy as jnp
from jax import lax
from jax.sharding import PartitionSpec as P

CB = 8
RS = 4


def to_tiles(matrix):
    points, row_count, order_size = matrix.shape
    tile_width = order_size // CB
    tile_rows = row_count // RS
    return (
        matrix.reshape(points, RS, tile_rows, CB, tile_width)
        .transpose(0, 1, 3, 2, 4)
        .reshape(points * RS * CB, tile_rows, tile_width)
    )


def from_tiles(tile_stack, points):
    total_tiles, tile_rows, tile_width = tile_stack.shape
    return (
        tile_stack.reshape(points, RS, CB, tile_rows, tile_width)
        .transpose(0, 1, 3, 2, 4)
        .reshape(points, RS * tile_rows, CB * tile_width)
    )


def scale_columns(left_side, column_scale):
    return (left_side.astype(jnp.float32) * column_scale[:, None, :]).astype(jnp.bfloat16)


def product_adder(scaled, shard_piece):
    return jnp.einsum("qij,qjk->qik", scaled, shard_piece, preferred_element_type=jnp.float32)


def pack_slots(tile_stack, slot_of_item, slot_total):
    item_total = tile_stack.shape[0]
    matches = (slot_of_item[None, :] == jnp.arange(slot_total, dtype=jnp.int32)[:, None]).astype(
        jnp.int32
    )
    item_index = jnp.sum(matches * jnp.arange(item_total, dtype=jnp.int32)[None, :], axis=1)
    filled = jnp.sum(matches, axis=1).astype(tile_stack.dtype)
    return jnp.take(tile_stack, item_index, axis=0) * filled[:, None, None]


def local(gamma_ph, full_ph, chi_ph, pp_vertex, chi_pp, relabel):
    points = gamma_ph.shape[0]
    nboson = lax.axis_size("boson")
    boson_here = lax.axis_index("boson")
    block_here = lax.axis_index("block")
    item_total = points * RS * CB
    capacity = -(-item_total // nboson) + 1
    phi_ph = product_adder(
        scale_columns(gamma_ph, chi_ph), lax.all_gather(full_ph, "block", axis=1, tiled=True)
    )
    ph_tiles = to_tiles(phi_ph.astype(jnp.bfloat16))
    tile_shape = ph_tiles.shape[1:]
    own_targets = lax.dynamic_slice(
        relabel, (boson_here * points, block_here * RS, 0), (points, RS, CB)
    ).reshape(item_total)
    shifts = (own_targets // points - boson_here) % nboson
    item_range = jnp.arange(item_total, dtype=jnp.int32)
    target = own_targets % points * (RS * CB) + item_range % (RS * CB)
    gather_order = jnp.sum(
        (target[None, :] == item_range[:, None]).astype(jnp.int32) * item_range[None, :], axis=1
    )
    earlier = (shifts[None, :] == shifts[:, None]) & (item_range[None, :] < item_range[:, None])
    slot_rank = jnp.sum(earlier.astype(jnp.int32), axis=1)
    send_slot = (boson_here + shifts) % nboson * capacity + slot_rank
    recv_slot = (boson_here - shifts) % nboson * capacity + slot_rank
    outgoing = pack_slots(ph_tiles, send_slot, nboson * capacity).reshape(
        (nboson, capacity) + tile_shape
    )
    incoming = lax.all_to_all(outgoing, "boson", split_axis=0, concat_axis=0, tiled=True).reshape(
        (nboson * capacity,) + tile_shape
    )
    arrived = jnp.take(incoming, recv_slot, axis=0)
    relabelled = from_tiles(jnp.take(arrived, gather_order, axis=0), points)
    phi_pp = product_adder(
        scale_columns(relabelled, chi_pp), lax.all_gather(pp_vertex, "block", axis=1, tiled=True)
    ).astype(jnp.bfloat16)
    leaving = jnp.take(to_tiles(phi_pp), target, axis=0)
    outgoing_back = pack_slots(leaving, recv_slot, nboson * capacity).reshape(
        (nboson, capacity) + tile_shape
    )
    incoming_back = lax.all_to_all(
        outgoing_back, "boson", split_axis=0, concat_axis=0, tiled=True
    ).reshape((nboson * capacity,) + tile_shape)
    returned = jnp.take(incoming_back, send_slot, axis=0)
    output = (
        gamma_ph.astype(jnp.float32) + phi_ph + from_tiles(returned, points).astype(jnp.float32)
    )
    return output.astype(jnp.bfloat16)


def solution(mesh):
    placed = (
        P("boson", "block", None),
        P("boson", "block", None),
        P("boson", None),
        P("boson", "block", None),
        P("boson", None),
        P(),
    )
    return jax.shard_map(
        local, mesh=mesh, in_specs=placed, out_specs=P("boson", "block", None), check_vma=False
    )
```

profile of v0, /device:TPU:0, one launch (start us, length us, event | category | flops | bytes accessed | tf_op | source)
XLA Modules:
  0.0 260.7 jit_solution(9437787763903134914)
XLA Ops:
  6.5 0.0 copy-start
  6.5 0.0 copy-start.2
  6.5 0.0 copy-start.4
  6.5 0.0 all-gather.3.cloned.1.call-start
  6.5 0.7 all-gather.3.cloned.1.call-update
  7.3 0.0 all-gather.5.cloned.1.call-start
  7.3 0.7 all-gather.5.cloned.1.call-update
  8.0 0.0 copy-done
  8.0 0.1 constant_dynamic-slice_fusion
  8.1 0.1 copy.17
  8.2 0.1 reshape.226
  8.3 0.2 convert_reduce_fusion.2
  8.6 0.2 convert_reduce_fusion
  8.8 61.1 %all-gather.3.cloned.1.call-done = bf16[4,1024,1024]{2,1,0:T(8,128)(2,1)} async-done(((bf16[4,256,1024]{2,1,0:T(8,128)(2,1)}), bf16[4,1024,1024]{2,1,0:T(8,128)(2,1)}) %all-gather.3.cloned.1.call-update) | async-done | bytes 8388624 | tf_op jit(solution)/shard_map/all_gather | solution.py:56
  69.9 0.0 copy-done.2
  69.9 0.0 copy-done.4
  69.9 7.7 %fusion.22 = (bf16[4,256,1024]{2,1,0:T(8,128)(2,1)S(1)}, f32[4,256,1024]{2,1,0:T(8,128)}) fusion(bf16[4,1024,1024]{2,1,0:T(8,128)(2,1)} %all-gather.3.cloned.1.call-done, bf16[4,256,1024]{2,1,0:T(8,128)(2,1)S(1)} %copy-done.2, f32[4,1024]{1,0:T(4,128)S(1)} %copy-done.4), kind=kOutput, calls=%fused_computation.79 | convolution fusion | flops 2151677952 | bytes 16793600 | tf_op jit(solution)/shard_map/qij,qjk->qik/dot_general | solution.py:35
  77.6 0.6 copy.22
  78.2 0.6 copy.18
  78.8 2.4 gather_fusion
  81.3 3.5 %select_multiply_fusion.1 = bf16[136,64,128]{2,1,0:T(8,128)(2,1)} fusion(bf16[136,64,128]{2,1,0:T(8,128)(2,1)} %gather_fusion, pred[136]{0:T(512)(128)(4,1)S(1)} %compare_and_fusion.5, bf16[136]{0:T(256)(128)(2,1)S(1)} %convert_element_type.72), kind=kLoop, calls=%fused_computation.15 | loop fusion | flops 2228224 | bytes 4456856 | tf_op jit(solution)/shard_map/mul | solution.py:45
  84.8 5.3 %all-to-all-start = ((bf16[8,17,64,128]{3,2,1,0:T(8,128)(2,1)}), bf16[8,17,64,128]{3,2,1,0:T(8,128)(2,1)S(1)}, u32[]{:S(2)}, u32[]{:S(2)}) async-start(bf16[8,17,64,128]{3,2,1,0:T(8,128)(2,1)} %bitcast.2), calls=%async_computation | async-start | bytes 4456448 | tf_op jit(solution)/shard_map/all_to_all | solution.py:76
  90.1 0.1 select_reduce_fusion.2
  90.3 51.2 %all-to-all-done = bf16[8,17,64,128]{3,2,1,0:T(8,128)(2,1)S(1)} async-done(((bf16[8,17,64,128]{3,2,1,0:T(8,128)(2,1)}), bf16[8,17,64,128]{3,2,1,0:T(8,128)(2,1)S(1)}, u32[]{:S(2)}, u32[]{:S(2)}) %all-to-all-start) | async-done | bytes 2228256 | tf_op jit(solution)/shard_map/all_to_all | solution.py:76
  141.6 2.1 gather_fusion.1
  143.7 1.9 broadcast_select_fusion.3
  145.6 2.1 gather_fusion.2
  147.7 1.9 broadcast_select_fusion.2
  149.6 0.5 convert_bitcast_fusion.1
  150.1 5.2 %copy.19 = f32[4,4,64,8,128]{4,3,2,1,0:T(8,128)} copy(f32[4,4,64,8,128]{4,2,3,1,0:T(8,128)S(1)} %convert_bitcast_fusion.1) | data formatting | bytes 8388608 | tf_op jit(solution)/shard_map/convert_element_type | solution.py:31
  155.3 0.0 copy-start.5
  155.3 4.9 %reshape.233 = f32[4,256,1024]{2,1,0:T(8,128)} reshape(f32[4,4,64,8,128]{4,3,2,1,0:T(8,128)} %copy.19) | data formatting | bytes 8388608 | tf_op jit(solution)/shard_map/convert_element_type | solution.py:31
  160.2 0.0 all-gather.5.cloned.1.call-done
  160.2 0.0 copy-done.5
  160.2 7.0 %fusion.8 = bf16[4,256,1024]{2,1,0:T(8,128)(2,1)S(1)} fusion(bf16[4,1024,1024]{2,1,0:T(8,128)(2,1)} %all-gather.5.cloned.1.call-done, f32[4,256,1024]{2,1,0:T(8,128)} %reshape.233, f32[4,1024]{1,0:T(4,128)S(1)} %copy-done.5), kind=kOutput, calls=%fused_computation.24 | convolution fusion | flops 2150629376 | bytes 14696448 | tf_op jit(solution)/shard_map/qij,qjk->qik/dot_general | solution.py:35
  167.2 0.6 copy.23
  167.8 0.6 copy.20
  168.4 2.1 gather_fusion.3
  170.6 1.9 broadcast_select_fusion.1
  172.4 2.4 gather_fusion.4
  174.8 3.2 %select_multiply_fusion = bf16[136,64,128]{2,1,0:T(8,128)(2,1)} fusion(bf16[136,64,128]{2,1,0:T(8,128)(2,1)} %gather_fusion.4, pred[136]{0:T(512)(128)(4,1)S(1)} %compare_and_fusion.1, bf16[136]{0:T(256)(128)(2,1)S(1)} %convert_element_type.80), kind=kLoop, calls=%fused_computation.14 | loop fusion | flops 2228224 | bytes 4456856 | tf_op jit(solution)/shard_map/mul | solution.py:45
  178.0 3.8 %all-to-all-start.1 = ((bf16[8,17,64,128]{3,2,1,0:T(8,128)(2,1)}), bf16[8,17,64,128]{3,2,1,0:T(8,128)(2,1)S(1)}, u32[]{:S(2)}, u32[]{:S(2)}) async-start(bf16[8,17,64,128]{3,2,1,0:T(8,128)(2,1)} %bitcast.8), calls=%async_computation.1 | async-start | bytes 4456448 | tf_op jit(solution)/shard_map/all_to_all | solution.py:88
  181.9 51.1 %all-to-all-done.1 = bf16[8,17,64,128]{3,2,1,0:T(8,128)(2,1)S(1)} async-done(((bf16[8,17,64,128]{3,2,1,0:T(8,128)(2,1)}), bf16[8,17,64,128]{3,2,1,0:T(8,128)(2,1)S(1)}, u32[]{:S(2)}, u32[]{:S(2)}) %all-to-all-start.1) | async-done | bytes 2228256 | tf_op jit(solution)/shard_map/all_to_all | solution.py:88
  233.0 2.1 gather_fusion.5
  235.1 1.9 broadcast_select_fusion
  237.0 0.5 convert_bitcast_fusion
  237.4 5.3 %copy.21 = f32[4,4,64,8,128]{4,3,2,1,0:T(8,128)} copy(f32[4,4,64,8,128]{4,2,3,1,0:T(8,128)S(1)} %convert_bitcast_fusion) | data formatting | bytes 8388608 | tf_op jit(solution)/shard_map/convert_element_type | solution.py:93
  242.7 0.0 copy-start.3
  242.7 5.0 %reshape.234 = f32[4,256,1024]{2,1,0:T(8,128)} reshape(f32[4,4,64,8,128]{4,3,2,1,0:T(8,128)} %copy.21) | data formatting | bytes 8388608 | tf_op jit(solution)/shard_map/convert_element_type | solution.py:93
  247.7 0.0 copy-done.3
  247.7 0.0 copy-start.1
  247.7 6.1 %fusion.2 = bf16[4,256,1024]{2,1,0:T(8,128)(2,1)} fusion(f32[4,256,1024]{2,1,0:T(8,128)} %reshape.234, f32[4,256,1024]{2,1,0:T(8,128)} %get-tuple-element.21, bf16[4,256,1024]{2,1,0:T(8,128)(2,1)S(1)} %copy-done.3), kind=kLoop, calls=%fused_computation.10 | loop fusion | flops 4194304 | bytes 12582912 | tf_op jit(solution)/shard_map/convert_element_type | solution.py:95
  253.8 0.0 copy-done.1
  (20 shorter events, 0.2 us)
Async XLA Ops:
  6.5 1.5 copy-start
  6.5 63.4 %copy-start.2 = (bf16[4,256,1024]{2,1,0:T(8,128)(2,1)S(1)}, bf16[4,256,1024]{2,1,0:T(8,128)(2,1)}, u32[]{:S(2)}) copy-start(bf16[4,256,1024]{2,1,0:T(8,128)(2,1)} %param.12) | copy-start | bytes 6291460
  6.5 63.4 %copy-start.4 = (f32[4,1024]{1,0:T(4,128)S(1)}, f32[4,1024]{1,0:T(4,128)}, u32[]{:S(2)}) copy-start(f32[4,1024]{1,0:T(4,128)} %param.14) | copy-start | bytes 49156
  6.5 63.4 %all-gather.3.cloned.1.call-start = ((), (), s32[]{:S(2)}) async-start(), calls=%async_computation.2 | async-start | bytes 10485760 | tf_op jit(solution)/shard_map/all_gather | solution.py:56
  7.3 152.9 %all-gather.5.cloned.1.call-start = ((), (), s32[]{:S(2)}) async-start(), calls=%async_computation.3 | async-start | bytes 10485760 | tf_op jit(solution)/shard_map/all_gather | solution.py:82
  84.8 56.8 %all-to-all-start = ((bf16[8,17,64,128]{3,2,1,0:T(8,128)(2,1)}), bf16[8,17,64,128]{3,2,1,0:T(8,128)(2,1)S(1)}, u32[]{:S(2)}, u32[]{:S(2)}) async-start(bf16[8,17,64,128]{3,2,1,0:T(8,128)(2,1)} %bitcast.2), calls=%async_computation | async-start | bytes 4456448 | tf_op jit(solution)/shard_map/all_to_all | solution.py:76
  155.3 4.9 %copy-start.5 = (f32[4,1024]{1,0:T(4,128)S(1)}, f32[4,1024]{1,0:T(4,128)}, u32[]{:S(2)}) copy-start(f32[4,1024]{1,0:T(4,128)} %param.16) | copy-start | bytes 49156
  178.0 54.9 %all-to-all-start.1 = ((bf16[8,17,64,128]{3,2,1,0:T(8,128)(2,1)}), bf16[8,17,64,128]{3,2,1,0:T(8,128)(2,1)S(1)}, u32[]{:S(2)}, u32[]{:S(2)}) async-start(bf16[8,17,64,128]{3,2,1,0:T(8,128)(2,1)} %bitcast.8), calls=%async_computation.1 | async-start | bytes 4456448 | tf_op jit(solution)/shard_map/all_to_all | solution.py:88
  242.7 5.0 %copy-start.3 = (bf16[4,256,1024]{2,1,0:T(8,128)(2,1)S(1)}, bf16[4,256,1024]{2,1,0:T(8,128)(2,1)}, u32[]{:S(2)}) copy-start(bf16[4,256,1024]{2,1,0:T(8,128)(2,1)} %param.12) | copy-start | bytes 6291460
  247.7 6.1 %copy-start.1 = (s32[32,16,8]{0,2,1:T(8,128)S(1)}, s32[32,16,8]{0,2,1:T(8,128)}, u32[]{:S(2)}) copy-start(s32[32,16,8]{0,2,1:T(8,128)} %param.17) | copy-start | bytes 49156
Sparse Core Ops, SparseCore 0:
  8.9 60.9 all-gather.2
  71.5 58.2 all-gather.4
where the time goes:
time: 261 us
  waiting for transfers between devices  165 us (63%)
  local copies, waits for them, and re-layouts  36.5 us (14%)
  other arithmetic  21.8 us (8%)
  matrix products  14.7 us (6%)
  between operations  13.7 us (5%)
  starting transfers between devices  9.13 us (3%)
    all_gather x1, waiting for transfers between devices, local(): lax.all_gather(full_ph, 'block', axis=1, tiled=True)  61.1 us
    all_to_all x1, waiting for transfers between devices, local(): lax.all_to_all(outgoing, 'boson', split_axis=0, concat_axis=0, tiled=True)  51.2 us
    all_to_all x1, waiting for transfers between devices, local(): lax.all_to_all(outgoing_back, 'boson', split_axis=0, concat_axis=0, tiled...  51.1 us
    dot_general x2, matrix products, product_adder(): jnp.einsum('qij,qjk->qik', scaled, shard_piece, preferred_element_type=jn...  14.7 us
    convert_element_type x2, local copies, waits for them, and re-layouts, local(): from_tiles(returned, points).astype(jnp.float32)  10.3 us
    convert_element_type x2, local copies, waits for them, and re-layouts, scale_columns(): left_side.astype(jnp.float32) * column_scale[:, None, :]  10.1 us
    mul x2, other arithmetic, pack_slots(): return jnp.take(tile_stack, item_index, axis=0) * filled[:, None, None]  6.72 us
    convert_element_type x1, other arithmetic, local(): return output.astype(jnp.bfloat16)  6.07 us
  transfers between devices with their start and end apart: 4, of which 3 were waited for; matrix products, arithmetic and copies ran while one was open for 13% of the time, Pallas kernels for 0%

commit v1 on v0

v1 whole, which is shorter than its diff:
```python
import functools
import jax
import jax.numpy as jnp
from jax import lax
from jax.experimental import pallas as pl
from jax.experimental.pallas import tpu as pltpu
from jax.sharding import PartitionSpec as P

MESH = pl.DeviceIdType.MESH
DMA = pltpu.SemaphoreType.DMA


class Gather:
    def __init__(self, nblock, shard, whole, bounce, sems):
        self.nblock, self.shard, self.whole, self.bounce = nblock, shard, whole, bounce
        self.far_s, self.far_r, self.near_s, self.near_r, self.fwd_s, self.fwd_r, self.loc = sems
        self.points, self.rows = shard.shape[0], shard.shape[1]
        self.boson = lax.axis_index("boson")
        self.here = lax.axis_index("block")
        self.partner = self.here + 1 - 2 * (self.here % 2)

    def peers(self):
        out = [self.partner]
        for j in range(1, self.nblock // 2):
            out.append((self.here + 2 * j) % self.nblock)
        return out

    def place(self, q, owner):
        return self.whole.at[q, pl.ds(pl.multiple_of(owner * self.rows, self.rows), self.rows)]

    def far(self, q, j, owner):
        return pltpu.make_async_remote_copy(
            src_ref=self.shard.at[q], dst_ref=self.place(q, owner),
            send_sem=self.far_s.at[j - 1, q], recv_sem=self.far_r.at[j - 1, q],
            device_id=(self.boson, (self.here + 2 * j) % self.nblock), device_id_type=MESH)

    def near(self, q, owner):
        return pltpu.make_async_remote_copy(
            src_ref=self.shard.at[q], dst_ref=self.place(q, owner),
            send_sem=self.near_s.at[q], recv_sem=self.near_r.at[q],
            device_id=(self.boson, self.partner), device_id_type=MESH)

    def forward(self, q, j, owner):
        return pltpu.make_async_remote_copy(
            src_ref=self.place(q, owner), dst_ref=self.place(q, owner),
            send_sem=self.fwd_s.at[j - 1, q], recv_sem=self.fwd_r.at[j - 1, q],
            device_id=(self.boson, self.partner), device_id_type=MESH)

    def local_in(self):
        return pltpu.make_async_copy(self.shard, self.bounce, self.loc.at[0])

    def local_out(self):
        rows = pl.ds(pl.multiple_of(self.here * self.rows, self.rows), self.rows)
        return pltpu.make_async_copy(self.bounce, self.whole.at[:, rows], self.loc.at[1])

    def start(self):
        for q in range(self.points):
            for j in range(1, self.nblock // 2):
                self.far(q, j, self.here).start()
        for q in range(self.points):
            self.near(q, self.here).start()
        self.local_in().start()

    def relay(self):
        self.local_in().wait()
        self.local_out().start()
        for q in range(self.points):
            for j in range(1, self.nblock // 2):
                owner = (self.here + self.nblock - 2 * j) % self.nblock
                self.far(q, j, owner).wait_recv()
                self.forward(q, j, owner).start()

    def finish(self):
        self.local_out().wait()
        for q in range(self.points):
            self.near(q, self.here).wait_send()
            self.near(q, self.partner).wait_recv()
            for j in range(1, self.nblock // 2):
                owner = (self.here + self.nblock - 2 * j) % self.nblock
                twin = (self.partner + self.nblock - 2 * j) % self.nblock
                self.far(q, j, self.here).wait_send()
                self.forward(q, j, owner).wait_send()
                self.forward(q, j, twin).wait_recv()


def gather_scratch(nblock, shard):
    far = max(nblock // 2 - 1, 1)
    points = shard.shape[0]
    return [
        pltpu.VMEM(shard.shape, shard.dtype),
        DMA((far, points)), DMA((far, points)), DMA((points,)), DMA((points,)),
        DMA((far, points)), DMA((far, points)), DMA((2,)),
    ]


class Exchange:
    def __init__(self, nboson, outgoing, incoming, bounce, send, recv, loc):
        self.n, self.outgoing, self.incoming, self.bounce = nboson, outgoing, incoming, bounce
        self.send, self.recv, self.loc = send, recv, loc
        self.boson = lax.axis_index("boson")
        self.block = lax.axis_index("block")

    def peers(self):
        return [(self.boson + s) % self.n for s in range(1, self.n)]

    def copy(self, s, slot):
        dest = (self.boson + s) % self.n
        return pltpu.make_async_remote_copy(
            src_ref=self.outgoing.at[dest], dst_ref=self.incoming.at[slot],
            send_sem=self.send.at[s], recv_sem=self.recv.at[s],
            device_id=(dest, self.block), device_id_type=MESH)

    def local_in(self):
        return pltpu.make_async_copy(self.outgoing.at[self.boson], self.bounce, self.loc.at[0])

    def local_out(self):
        return pltpu.make_async_copy(self.bounce, self.incoming.at[self.boson], self.loc.at[1])

    def order(self):
        mid = self.n // 2
        return sorted(range(1, self.n), key=lambda s: (abs(s - mid), s))

    def start(self):
        for s in self.order():
            self.copy(s, self.boson).start()
        self.local_in().start()

    def finish(self):
        self.local_in().wait()
        self.local_out().start()
        for s in self.order():
            self.copy(s, self.boson).wait_send()
            self.copy(s, (self.boson + self.n - s) % self.n).wait_recv()
        self.local_out().wait()


def exchange_scratch(nboson, outgoing):
    return [
        pltpu.VMEM(outgoing.shape[1:], outgoing.dtype),
        DMA((nboson,)), DMA((nboson,)), DMA((2,)),
    ]


def greet(block_peers, boson_peers):
    barrier = pltpu.get_barrier_semaphore()
    boson, block = lax.axis_index("boson"), lax.axis_index("block")
    for peer in block_peers:
        pl.semaphore_signal(barrier, inc=1, device_id=(boson, peer), device_id_type=MESH)
    for peer in boson_peers:
        pl.semaphore_signal(barrier, inc=1, device_id=(peer, block), device_id_type=MESH)
    pl.semaphore_wait(barrier, len(block_peers) + len(boson_peers))


def gather_kernel(nblock, shard, whole, bounce, *sems):
    gather = Gather(nblock, shard, whole, bounce, sems)
    greet(gather.peers(), [])
    gather.start()
    gather.relay()
    gather.finish()


def both_kernel(nblock, nboson, shard, outgoing, whole, incoming, *scratch):
    gather = Gather(nblock, shard, whole, scratch[0], scratch[1:8])
    exchange = Exchange(nboson, outgoing, incoming, *scratch[8:])
    greet(gather.peers(), exchange.peers())
    exchange.start()
    gather.start()
    gather.relay()
    gather.finish()
    exchange.finish()


def exchange_kernel(nboson, outgoing, incoming, *scratch):
    exchange = Exchange(nboson, outgoing, incoming, *scratch)
    greet([], exchange.peers())
    exchange.start()
    exchange.finish()


ANY = pl.BlockSpec(memory_space=pl.ANY)


def remote_call(body, operands, outs, scratch, ident, name):
    return pl.pallas_call(
        body, out_shape=outs, in_specs=[ANY] * len(operands),
        out_specs=jax.tree.map(lambda _: ANY, outs), scratch_shapes=scratch, name=name,
        compiler_params=pltpu.CompilerParams(collective_id=ident, has_side_effects=True),
    )(*operands)


def row_of(chi, index):
    rows = lax.broadcasted_iota(jnp.int32, chi.shape, 0)
    return jnp.sum(jnp.where(rows == index, chi[...], 0.0), axis=0, keepdims=True)


def first_kernel(row_tiles, col_blocks, slots, gamma, chi, full, packed, base, scaled):
    q = pl.program_id(0)
    rows, order = gamma.shape[1], gamma.shape[2]
    high, wide = rows // row_tiles, order // col_blocks
    scaled[...] = (gamma[0].astype(jnp.float32) * row_of(chi, q)).astype(jnp.bfloat16)
    step = 2 * wide
    for start in range(0, order, step):
        phi = jnp.dot(scaled[...], full[0, :, start:start + step],
                      preferred_element_type=jnp.float32)
        base[0, :, start:start + step] = gamma[0, :, start:start + step].astype(jnp.float32) + phi
        wire = phi.astype(jnp.bfloat16)
        for r in range(row_tiles):
            for k in range(2):
                item = (q * row_tiles + r) * col_blocks + start // wide + k
                packed[slots[item]] = wire[r * high:(r + 1) * high, k * wide:(k + 1) * wide]


def second_kernel(row_tiles, col_blocks, slots, arrived, chi, full, packed, scaled):
    p = pl.program_id(0)
    rows, order = scaled.shape
    high, wide = rows // row_tiles, order // col_blocks
    chi_row = row_of(chi, p)
    for c in range(col_blocks):
        chi_c = chi_row[:, c * wide:(c + 1) * wide]
        for r in range(row_tiles):
            tile = arrived[slots[(p * row_tiles + r) * col_blocks + c]]
            scaled[r * high:(r + 1) * high, c * wide:(c + 1) * wide] = (
                tile.astype(jnp.float32) * chi_c).astype(jnp.bfloat16)
    step = 2 * wide
    for start in range(0, order, step):
        wire = jnp.dot(scaled[...], full[0, :, start:start + step],
                       preferred_element_type=jnp.float32).astype(jnp.bfloat16)
        for r in range(row_tiles):
            for k in range(2):
                item = (p * row_tiles + r) * col_blocks + start // wide + k
                packed[slots[item]] = wire[r * high:(r + 1) * high, k * wide:(k + 1) * wide]


def last_kernel(row_tiles, col_blocks, slots, arrived, base, out):
    q = pl.program_id(0)
    rows, order = out.shape[1], out.shape[2]
    high, wide = rows // row_tiles, order // col_blocks
    for r in range(row_tiles):
        for c in range(col_blocks):
            tile = arrived[slots[(q * row_tiles + r) * col_blocks + c]]
            place = (0, slice(r * high, (r + 1) * high), slice(c * wide, (c + 1) * wide))
            out[place] = (base[place] + tile.astype(jnp.float32)).astype(jnp.bfloat16)


def point_spec(shape):
    return pl.BlockSpec((1,) + tuple(shape[1:]), lambda i, *_: (i, 0, 0))


def whole_spec(shape):
    return pl.BlockSpec(tuple(shape), lambda i, *_: (0,) * len(shape))


def tables(relabel, points, row_tiles, nboson, capacity):
    boson, block = lax.axis_index("boson"), lax.axis_index("block")
    col_blocks = relabel.shape[2]
    per_point = row_tiles * col_blocks
    total = points * per_point
    own = lax.dynamic_slice(
        relabel, (boson * points, block * row_tiles, 0), (points, row_tiles, col_blocks)
    ).reshape(total)
    shifts = (own // points - boson) % nboson
    items = jnp.arange(total, dtype=jnp.int32)
    target = own % points * per_point + items % per_point
    earlier = (shifts[None, :] == shifts[:, None]) & (items[None, :] < items[:, None])
    rank = jnp.sum(earlier.astype(jnp.int32), axis=1)
    send_slot = (boson + shifts) % nboson * capacity + rank
    recv_slot = (boson - shifts) % nboson * capacity + rank
    hit = (target[None, :] == items[:, None]).astype(jnp.int32)
    back_slot = jnp.sum(hit * recv_slot[None, :], axis=1)
    return send_slot, back_slot


def local(nboson, nblock, gamma_ph, full_ph, chi_ph, pp_vertex, chi_pp, relabel):
    points, rows, order = gamma_ph.shape
    row_tiles, col_blocks = relabel.shape[1] // nblock, relabel.shape[2]
    high, wide = rows // row_tiles, order // col_blocks
    capacity = -(-(points * row_tiles * col_blocks) // nboson) + 1
    send_slot, back_slot = tables(relabel, points, row_tiles, nboson, capacity)
    shape = jax.ShapeDtypeStruct
    bf16, f32 = jnp.bfloat16, jnp.float32
    whole = shape((points, order, order), bf16)
    packed = shape((nboson * capacity, high, wide), bf16)
    slabs = shape((nboson, capacity, high, wide), bf16)
    scaled = pltpu.VMEM((rows, order), bf16)

    full = remote_call(
        functools.partial(gather_kernel, nblock), (full_ph,), whole,
        gather_scratch(nblock, full_ph), 0, "gather_full")
    outgoing, base = pl.pallas_call(
        functools.partial(first_kernel, row_tiles, col_blocks),
        out_shape=(packed, shape(gamma_ph.shape, f32)), name="first",
        grid_spec=pltpu.PrefetchScalarGridSpec(
            num_scalar_prefetch=1, grid=(points,),
            in_specs=[point_spec(gamma_ph.shape), whole_spec(chi_ph.shape), point_spec(whole.shape)],
            out_specs=(whole_spec(packed.shape), point_spec(gamma_ph.shape)),
            scratch_shapes=[scaled]),
    )(send_slot, gamma_ph, chi_ph, full)
    pp_full, incoming = remote_call(
        functools.partial(both_kernel, nblock, nboson),
        (pp_vertex, outgoing.reshape(slabs.shape)), (whole, slabs),
        gather_scratch(nblock, pp_vertex) + exchange_scratch(nboson, slabs), 1, "both")
    outgoing_back = pl.pallas_call(
        functools.partial(second_kernel, row_tiles, col_blocks),
        out_shape=packed, name="second",
        grid_spec=pltpu.PrefetchScalarGridSpec(
            num_scalar_prefetch=1, grid=(points,),
            in_specs=[whole_spec(packed.shape), whole_spec(chi_pp.shape), point_spec(whole.shape)],
            out_specs=whole_spec(packed.shape), scratch_shapes=[scaled]),
    )(back_slot, incoming.reshape(packed.shape), chi_pp, pp_full)
    incoming_back = remote_call(
        functools.partial(exchange_kernel, nboson), (outgoing_back.reshape(slabs.shape),), slabs,
        exchange_scratch(nboson, slabs), 2, "back")
    return pl.pallas_call(
        functools.partial(last_kernel, row_tiles, col_blocks),
        out_shape=shape(gamma_ph.shape, bf16), name="last",
        grid_spec=pltpu.PrefetchScalarGridSpec(
            num_scalar_prefetch=1, grid=(points,),
            in_specs=[whole_spec(packed.shape), point_spec(gamma_ph.shape)],
            out_specs=point_spec(gamma_ph.shape)),
    )(send_slot, incoming_back.reshape(packed.shape), base)


def solution(mesh):
    placed = (
        P("boson", "block", None),
        P("boson", "block", None),
        P("boson", None),
        P("boson", "block", None),
        P("boson", None),
        P(),
    )
    return jax.shard_map(
        functools.partial(local, mesh.shape["boson"], mesh.shape["block"]), mesh=mesh,
        in_specs=placed, out_specs=P("boson", "block", None), check_vma=False,
    )
```

time: 261 us -> 182 us (0.70)
  the two profiles are of different devices: /device:TPU:0 before, /device:TPU:17 now
where the time goes in v1:
time: 182 us
  Pallas kernels  179 us (98%)
    pallas_call x3, Pallas kernels, remote_call(): pl.pallas_call(body, out_shape=outs, in_specs=[ANY] * len(operands), out_...  156 us
    pallas_call x1, Pallas kernels, local(): pl.pallas_call(functools.partial(first_kernel, row_tiles, col_blocks), ou...  9.04 us
    pallas_call x1, Pallas kernels, local(): pl.pallas_call(functools.partial(second_kernel, row_tiles, col_blocks), o...  8.32 us
    pallas_call x1, Pallas kernels, local(): pl.pallas_call(functools.partial(last_kernel, row_tiles, col_blocks), out...  5.74 us

profile of v1, /device:TPU:17, one launch (start us, length us, event | category | flops | bytes accessed | tf_op | source)
XLA Modules:
  0.0 181.8 jit_solution(4524667265443710056)
XLA Ops:
  0.0 0.0 copy-start
  0.0 0.8 copy-done
  0.8 0.1 constant_dynamic-slice_fusion
  0.9 0.1 copy.8
  1.0 0.1 reshape.152
  1.1 0.2 convert_reduce_fusion
  1.3 0.6 fusion.6
  1.9 0.6 select_reduce_fusion.slots
  2.5 50.8 %gather_full.1.full = bf16[4,1024,1024]{2,1,0:T(8,128)(2,1)} custom-call(bf16[4,256,1024]{2,1,0:T(8,128)(2,1)} %shard.2), custom_call_target="tpu_custom_call" | custom-call | tf_op jit(solution)/shard_map/gather_full/pallas_call | solution.py:184
  53.3 9.0 %first.1 = (bf16[136,64,128]{2,1,0:T(8,128)(2,1)}, f32[4,256,1024]{2,1,0:T(8,128)}) custom-call(s32[128]{0:T(128)} %get-tuple-element.14.slots, bf16[4,256,1024]{2,1,0:T(8,128)(2,1)} %gamma.1, f32[4,1024]{1,0:T(4,128)} %chi.2, bf16[4,1024,1024]{2,1,0:T(8,128)(2,1)} %gather_full.1.full), custom_call_target="tpu_custom_call" | custom-call | tf_op jit(solution)/shard_map/first/pallas_call | solution.py:289
  62.3 52.8 %both.1 = (bf16[4,1024,1024]{2,1,0:T(8,128)(2,1)}, bf16[8,17,64,128]{3,2,1,0:T(8,128)(2,1)}) custom-call(bf16[4,256,1024]{2,1,0:T(8,128)(2,1)} %shard.3, bf16[8,17,64,128]{3,2,1,0:T(8,128)(2,1)} %bitcast.7), custom_call_target="tpu_custom_call" | custom-call | tf_op jit(solution)/shard_map/both/pallas_call | solution.py:184
  115.1 8.3 %second.1 = bf16[136,64,128]{2,1,0:T(8,128)(2,1)} custom-call(s32[128]{0:T(128)} %select_reduce_fusion.slots, bf16[136,64,128]{2,1,0:T(8,128)(2,1)} %bitcast.6, f32[4,1024]{1,0:T(4,128)} %chi.3, bf16[4,1024,1024]{2,1,0:T(8,128)(2,1)} %get-tuple-element.11.full), custom_call_target="tpu_custom_call" | custom-call | tf_op jit(solution)/shard_map/second/pallas_call | solution.py:302
  123.4 52.6 %back.1 = bf16[8,17,64,128]{3,2,1,0:T(8,128)(2,1)} custom-call(bf16[8,17,64,128]{3,2,1,0:T(8,128)(2,1)} %bitcast.4), custom_call_target="tpu_custom_call" | custom-call | tf_op jit(solution)/shard_map/back/pallas_call | solution.py:184
  176.0 5.7 %last.1 = bf16[4,256,1024]{2,1,0:T(8,128)(2,1)} custom-call(s32[128]{0:T(128)} %get-tuple-element.14.slots, bf16[136,64,128]{2,1,0:T(8,128)(2,1)} %bitcast.5, f32[4,256,1024]{2,1,0:T(8,128)} %get-tuple-element.12.base), custom_call_target="tpu_custom_call" | custom-call | tf_op jit(solution)/shard_map/last/pallas_call | solution.py:313
  (1 shorter events, 0.0 us)
Async XLA Ops:
  0.0 0.8 copy-start

commit v2 on v0

v2 whole, which is shorter than its diff:
```python
import functools
import jax
import jax.numpy as jnp
from jax import lax
from jax.experimental import pallas as pl
from jax.experimental.pallas import tpu as pltpu
from jax.sharding import PartitionSpec as P

MESH = pl.DeviceIdType.MESH
DMA = pltpu.SemaphoreType.DMA
PARTS = 2


def loop(start, stop, body):
    lax.fori_loop(start, stop, lambda i, carry: (body(i), carry)[1], 0)


class Gather:
    def __init__(self, nblock, shard, whole, sems):
        self.nblock, self.shard, self.whole = nblock, shard, whole
        self.far_s, self.far_r, self.near_s, self.near_r, self.fwd_s, self.fwd_r, self.loc = sems
        self.points, self.rows, order = shard.shape
        self.cols = order // PARTS
        self.chunks = self.points * PARTS
        self.boson = lax.axis_index("boson")
        self.here = lax.axis_index("block")
        self.partner = self.here + 1 - 2 * (self.here % 2)

    def peers(self):
        out = [self.partner]
        for j in range(1, self.nblock // 2):
            out.append((self.here + 2 * j) % self.nblock)
        return out

    def columns(self, g):
        return pl.ds(pl.multiple_of(g % PARTS * self.cols, self.cols), self.cols)

    def source(self, g):
        return self.shard.at[g // PARTS, :, self.columns(g)]

    def place(self, g, owner):
        rows = pl.ds(pl.multiple_of(owner * self.rows, self.rows), self.rows)
        return self.whole.at[g // PARTS, rows, self.columns(g)]

    def far(self, g, j, owner):
        return pltpu.make_async_remote_copy(
            src_ref=self.source(g), dst_ref=self.place(g, owner),
            send_sem=self.far_s.at[j - 1, g], recv_sem=self.far_r.at[j - 1, g],
            device_id=(self.boson, (self.here + 2 * j) % self.nblock), device_id_type=MESH)

    def near(self, g, owner):
        return pltpu.make_async_remote_copy(
            src_ref=self.source(g), dst_ref=self.place(g, owner),
            send_sem=self.near_s.at[g], recv_sem=self.near_r.at[g],
            device_id=(self.boson, self.partner), device_id_type=MESH)

    def forward(self, g, j, owner):
        return pltpu.make_async_remote_copy(
            src_ref=self.place(g, owner), dst_ref=self.place(g, owner),
            send_sem=self.fwd_s.at[j - 1, g], recv_sem=self.fwd_r.at[j - 1, g],
            device_id=(self.boson, self.partner), device_id_type=MESH)

    def own(self):
        rows = pl.ds(pl.multiple_of(self.here * self.rows, self.rows), self.rows)
        return pltpu.make_async_copy(self.shard, self.whole.at[:, rows], self.loc)

    def each_far(self, act):
        for j in range(1, self.nblock // 2):
            act(j)

    def start(self):
        def one(g):
            self.each_far(lambda j: self.far(g, j, self.here).start())
            self.near(g, self.here).start()
        loop(0, self.chunks, one)

    def relay(self, g):
        def one(j):
            owner = (self.here + self.nblock - 2 * j) % self.nblock
            self.far(g, j, owner).wait_recv()
            self.forward(g, j, owner).start()
        self.each_far(one)

    def arrived(self, g):
        self.near(g, self.partner).wait_recv()
        def one(j):
            twin = (self.partner + self.nblock - 2 * j) % self.nblock
            self.forward(g, j, twin).wait_recv()
        self.each_far(one)

    def sent_far(self):
        loop(0, self.chunks,
             lambda g: self.each_far(lambda j: self.far(g, j, self.here).wait_send()))

    def sent_near(self):
        def one(g):
            self.near(g, self.here).wait_send()
            def fwd(j):
                owner = (self.here + self.nblock - 2 * j) % self.nblock
                self.forward(g, j, owner).wait_send()
            self.each_far(fwd)
        loop(0, self.chunks, one)


def gather_scratch(nblock, points):
    far, chunks = max(nblock // 2 - 1, 1), points * PARTS
    return [DMA((far, chunks)), DMA((far, chunks)), DMA((chunks,)), DMA((chunks,)),
            DMA((far, chunks)), DMA((far, chunks)), DMA]


class Exchange:
    def __init__(self, nboson, outgoing, incoming, send, recv):
        self.n, self.outgoing, self.incoming = nboson, outgoing, incoming
        self.send, self.recv = send, recv
        self.boson = lax.axis_index("boson")
        self.block = lax.axis_index("block")

    def peers(self):
        return [(self.boson + s) % self.n for s in range(1, self.n)]

    def shift(self, i):
        return self.n // 2 + (1 - 2 * (i % 2)) * ((i + 1) // 2)

    def copy(self, s, slot):
        dest = (self.boson + s) % self.n
        return pltpu.make_async_remote_copy(
            src_ref=self.outgoing.at[dest], dst_ref=self.incoming.at[slot],
            send_sem=self.send.at[s], recv_sem=self.recv.at[s],
            device_id=(dest, self.block), device_id_type=MESH)

    def pack(self, target, dest, tiles, table):
        capacity = target.shape[1]
        for k in range(capacity):
            target[dest, k] = tiles[table[dest * capacity + k]]

    def pack_and_start(self, tiles, table):
        def pack(i):
            self.pack(self.outgoing, (self.boson + self.shift(i)) % self.n, tiles, table)
        pack(0)
        def one(i):
            pack(i)
            self.copy(self.shift(i - 1), self.boson).start()
        loop(1, self.n - 1, one)
        self.pack(self.incoming, self.boson, tiles, table)
        self.copy(self.shift(self.n - 2), self.boson).start()

    def received(self):
        loop(1, self.n, lambda s: self.copy(s, (self.boson + self.n - s) % self.n).wait_recv())

    def sent(self):
        loop(1, self.n, lambda s: self.copy(s, self.boson).wait_send())


def greet(block_peers, boson_peers):
    barrier = pltpu.get_barrier_semaphore()
    boson, block = lax.axis_index("boson"), lax.axis_index("block")
    for peer in block_peers:
        pl.semaphore_signal(barrier, inc=1, device_id=(boson, peer), device_id_type=MESH)
    for peer in boson_peers:
        pl.semaphore_signal(barrier, inc=1, device_id=(peer, block), device_id_type=MESH)
    pl.semaphore_wait(barrier, len(block_peers) + len(boson_peers))


def kernel(nboson, nblock, row_tiles, col_blocks,
           send_slot, item_of, back_slot, back_item_of,
           gamma_in, full_in, chi_ph, pp_in, chi_pp, out,
           full, pp, gamma, scaled, base, tiles, packed, landed, back, returned, result,
           gamma_sem, out_sem, ahead_s, ahead_r, home_s, home_r, *gather_sems):
    half = len(gather_sems) // 2
    first = Gather(nblock, full_in, full, gather_sems[:half])
    second = Gather(nblock, pp_in, pp, gather_sems[half:])
    ahead = Exchange(nboson, packed, landed, ahead_s, ahead_r)
    home = Exchange(nboson, back, returned, home_s, home_r)
    points, rows, order = gamma.shape
    high, wide = rows // row_tiles, order // col_blocks
    step = 2 * wide
    load_gamma = pltpu.make_async_copy(gamma_in, gamma, gamma_sem)

    first.own().start()
    load_gamma.start()
    second.own().start()
    greet(first.peers(), ahead.peers())
    first.start()

    load_gamma.wait()
    for q in range(points):
        scaled[q] = (gamma[q].astype(jnp.float32) * chi_ph[q:q + 1, :]).astype(jnp.bfloat16)
    first.own().wait()

    def cut(wire, q, column):
        for r in range(row_tiles):
            for k in range(2):
                item = (q * row_tiles + r) * col_blocks + column * 2 + k
                tiles[item] = wire[r * high:(r + 1) * high, k * wide:(k + 1) * wide]

    def product(whole, q, column):
        at = pl.ds(pl.multiple_of(column * step, step), step)
        return at, jnp.dot(scaled[q], whole[q, :, at], preferred_element_type=jnp.float32)

    per_part = order // step // PARTS

    def compute(g):
        first.arrived(g)
        q = g // PARTS
        for n in range(per_part):
            column = g % PARTS * per_part + n
            at, phi = product(full, q, column)
            base[q, :, at] = gamma[q, :, at].astype(jnp.float32) + phi
            cut(phi.astype(jnp.bfloat16), q, column)

    first.relay(0)
    def one(g):
        first.relay(g)
        compute(g - 1)
    loop(1, first.chunks, one)
    first.sent_far()
    second.start()
    compute(first.chunks - 1)
    ahead.pack_and_start(tiles, item_of)

    loop(0, second.chunks, second.relay)
    first.sent_near()
    second.own().wait()
    loop(0, second.chunks, second.arrived)
    ahead.received()

    capacity = landed.shape[1]
    flat = landed.reshape(nboson * capacity, high, wide)
    for p in range(points):
        for c in range(col_blocks):
            chi = chi_pp[p:p + 1, c * wide:(c + 1) * wide]
            for r in range(row_tiles):
                tile = flat[back_slot[(p * row_tiles + r) * col_blocks + c]]
                scaled[p, r * high:(r + 1) * high, c * wide:(c + 1) * wide] = (
                    tile.astype(jnp.float32) * chi).astype(jnp.bfloat16)
    def point(p):
        for column in range(order // step):
            _, phi = product(pp, p, column)
            cut(phi.astype(jnp.bfloat16), p, column)
    loop(0, points, point)
    home.pack_and_start(tiles, back_item_of)
    ahead.sent()
    second.sent_far()
    second.sent_near()
    home.received()

    flat_back = returned.reshape(nboson * capacity, high, wide)
    def finish(q):
        for r in range(row_tiles):
            for c in range(col_blocks):
                tile = flat_back[send_slot[(q * row_tiles + r) * col_blocks + c]]
                at = (q, slice(r * high, (r + 1) * high), slice(c * wide, (c + 1) * wide))
                result[at] = (base[at] + tile.astype(jnp.float32)).astype(jnp.bfloat16)
        pltpu.make_async_copy(result.at[q], out.at[q], out_sem.at[q]).start()
    loop(0, points, finish)
    home.sent()
    loop(0, points,
         lambda q: pltpu.make_async_copy(result.at[q], out.at[q], out_sem.at[q]).wait())


def tables(relabel, points, row_tiles, nboson, capacity):
    boson, block = lax.axis_index("boson"), lax.axis_index("block")
    col_blocks = relabel.shape[2]
    per_point = row_tiles * col_blocks
    total = points * per_point
    own = lax.dynamic_slice(
        relabel, (boson * points, block * row_tiles, 0), (points, row_tiles, col_blocks)
    ).reshape(total)
    shifts = (own // points - boson) % nboson
    items = jnp.arange(total, dtype=jnp.int32)
    slots = jnp.arange(nboson * capacity, dtype=jnp.int32)
    target = own % points * per_point + items % per_point
    earlier = (shifts[None, :] == shifts[:, None]) & (items[None, :] < items[:, None])
    rank = jnp.sum(earlier.astype(jnp.int32), axis=1)
    send_slot = (boson + shifts) % nboson * capacity + rank
    recv_slot = (boson - shifts) % nboson * capacity + rank

    def pick(keys, wanted, values):
        hit = (keys[None, :] == wanted[:, None]).astype(jnp.int32)
        return jnp.sum(hit * values[None, :], axis=1)

    return (send_slot, pick(send_slot, slots, items), pick(target, items, recv_slot),
            pick(recv_slot, slots, target))


def local(nboson, nblock, gamma_ph, full_ph, chi_ph, pp_vertex, chi_pp, relabel):
    points, rows, order = gamma_ph.shape
    row_tiles, col_blocks = relabel.shape[1] // nblock, relabel.shape[2]
    high, wide = rows // row_tiles, order // col_blocks
    total = points * row_tiles * col_blocks
    capacity = -(-total // nboson) + 1
    bf16, f32 = jnp.bfloat16, jnp.float32
    whole = pltpu.VMEM((points, order, order), bf16)
    shard = pltpu.VMEM(gamma_ph.shape, bf16)
    slabs = pltpu.VMEM((nboson, capacity, high, wide), bf16)
    smem = pl.BlockSpec(memory_space=pltpu.SMEM)
    vmem = pl.BlockSpec(memory_space=pltpu.VMEM)
    hbm = pl.BlockSpec(memory_space=pl.ANY)
    return pl.pallas_call(
        functools.partial(kernel, nboson, nblock, row_tiles, col_blocks),
        out_shape=jax.ShapeDtypeStruct(gamma_ph.shape, bf16), name="window",
        in_specs=[smem] * 4 + [hbm, hbm, vmem, hbm, vmem], out_specs=hbm,
        scratch_shapes=[
            whole, whole, shard, shard, pltpu.VMEM(gamma_ph.shape, f32),
            pltpu.VMEM((total, high, wide), bf16), slabs, slabs, slabs, slabs, shard,
            DMA, DMA((points,)), DMA((nboson,)), DMA((nboson,)), DMA((nboson,)), DMA((nboson,)),
        ] + gather_scratch(nblock, points) + gather_scratch(nblock, points),
        compiler_params=pltpu.CompilerParams(
            collective_id=0, has_side_effects=True, vmem_limit_bytes=60 * 1024 * 1024),
    )(*tables(relabel, points, row_tiles, nboson, capacity),
      gamma_ph, full_ph, chi_ph, pp_vertex, chi_pp)


def solution(mesh):
    placed = (
        P("boson", "block", None),
        P("boson", "block", None),
        P("boson", None),
        P("boson", "block", None),
        P("boson", None),
        P(),
    )
    return jax.shard_map(
        functools.partial(local, mesh.shape["boson"], mesh.shape["block"]), mesh=mesh,
        in_specs=placed, out_specs=P("boson", "block", None), check_vma=False,
    )
```

time: 261 us -> 161 us (0.62)
  the two profiles are of different devices: /device:TPU:0 before, /device:TPU:17 now
where the time goes in v2:
time: 161 us; the launch traced here: 160 us
  Pallas kernels  155 us (96%)
  local copies, waits for them, and re-layouts  4.19 us (3%)
    pallas_call x1, Pallas kernels, local(): pl.pallas_call(functools.partial(kernel, nboson, nblock, row_tiles, col_b...  155 us
    unnamed x5, local copies, waits for them, and re-layouts  3.92 us

profile of v2, /device:TPU:17, one launch (start us, length us, event | category | flops | bytes accessed | tf_op | source)
XLA Modules:
  0.0 160.4 jit_solution(14941044209746416566)
XLA Ops:
  0.0 0.0 copy-start
  0.0 0.8 copy-done
  0.8 0.1 constant_dynamic-slice_fusion
  0.9 0.1 copy.8
  1.0 0.1 reshape.165
  1.1 0.2 convert_reduce_fusion
  1.3 0.0 copy-start.1
  1.3 0.6 select_reduce_fusion.2.back_slot
  2.0 0.7 select_reduce_fusion
  2.7 0.0 copy-done.1
  2.7 154.6 %window.1 = bf16[4,256,1024]{2,1,0:T(8,128)(2,1)} custom-call(s32[128]{0:T(128)} %copy-done.1, s32[136]{0:T(256)} %get-tuple-element.10.item_of, s32[128]{0:T(128)} %select_reduce_fusion.2.back_slot, s32[136]{0:T(256)} %get-tuple-element.9.back_item_of, bf16[4,256,1024]{2,1,0:T(8,128)(2,1)} %gamma_in.1, bf16[4,256,1024]{2,1,0:T(8,128)(2,1)} %full_in.1, ...), custom_call_target="tpu_custom_call" | custom-call | tf_op jit(solution)/shard_map/window/pallas_call | solution.py:299
  157.4 3.1 %copy.10 = bf16[4,256,1024]{2,1,0:T(8,128)(2,1)} copy(bf16[4,256,1024]{2,1,0:T(8,128)(2,1)} %window.1) | data formatting | bytes 4194304
  (2 shorter events, 0.0 us)
Async XLA Ops:
  0.0 0.8 copy-start
  1.3 1.4 copy-start.1

commit v3 on v2

--- a/solution.py
+++ b/solution.py
@@ -8,7 +8,7 @@
 
 MESH = pl.DeviceIdType.MESH
 DMA = pltpu.SemaphoreType.DMA
-PARTS = 2
+PARTS = 4
 
 
 def loop(start, stop, body):
@@ -164,8 +164,8 @@
 def kernel(nboson, nblock, row_tiles, col_blocks,
            send_slot, item_of, back_slot, back_item_of,
            gamma_in, full_in, chi_ph, pp_in, chi_pp, out,
-           full, pp, gamma, scaled, base, tiles, packed, landed, back, returned, result,
-           gamma_sem, out_sem, ahead_s, ahead_r, home_s, home_r, *gather_sems):
+           full, pp, gamma, scaled, base, tiles, packed, landed, back, returned,
+           gamma_sem, ahead_s, ahead_r, home_s, home_r, *gather_sems):
     half = len(gather_sems) // 2
     first = Gather(nblock, full_in, full, gather_sems[:half])
     second = Gather(nblock, pp_in, pp, gather_sems[half:])
@@ -250,12 +250,9 @@
             for c in range(col_blocks):
                 tile = flat_back[send_slot[(q * row_tiles + r) * col_blocks + c]]
                 at = (q, slice(r * high, (r + 1) * high), slice(c * wide, (c + 1) * wide))
-                result[at] = (base[at] + tile.astype(jnp.float32)).astype(jnp.bfloat16)
-        pltpu.make_async_copy(result.at[q], out.at[q], out_sem.at[q]).start()
+                out[at] = (base[at] + tile.astype(jnp.float32)).astype(jnp.bfloat16)
     loop(0, points, finish)
     home.sent()
-    loop(0, points,
-         lambda q: pltpu.make_async_copy(result.at[q], out.at[q], out_sem.at[q]).wait())
 
 
 def tables(relabel, points, row_tiles, nboson, capacity):
@@ -298,12 +295,12 @@
     hbm = pl.BlockSpec(memory_space=pl.ANY)
     return pl.pallas_call(
         functools.partial(kernel, nboson, nblock, row_tiles, col_blocks),
-        out_shape=jax.ShapeDtypeStruct(gamma_ph.shape, bf16), name="window",
-        in_specs=[smem] * 4 + [hbm, hbm, vmem, hbm, vmem], out_specs=hbm,
+        out_shape=pltpu.VMEM(gamma_ph.shape, bf16), name="window",
+        in_specs=[smem] * 4 + [hbm, hbm, vmem, hbm, vmem], out_specs=vmem,
         scratch_shapes=[
             whole, whole, shard, shard, pltpu.VMEM(gamma_ph.shape, f32),
-            pltpu.VMEM((total, high, wide), bf16), slabs, slabs, slabs, slabs, shard,
-            DMA, DMA((points,)), DMA((nboson,)), DMA((nboson,)), DMA((nboson,)), DMA((nboson,)),
+            pltpu.VMEM((total, high, wide), bf16), slabs, slabs, slabs, slabs,
+            DMA, DMA((nboson,)), DMA((nboson,)), DMA((nboson,)), DMA((nboson,)),
         ] + gather_scratch(nblock, points) + gather_scratch(nblock, points),
         compiler_params=pltpu.CompilerParams(
             collective_id=0, has_side_effects=True, vmem_limit_bytes=60 * 1024 * 1024),

time: 161 us -> 159 us (0.988)
  local copies, waits for them, and re-layouts: 4.19 us -> 2.43 us
    unnamed x5, local copies, waits for them, and re-layouts: 3.92 us -> 2.17 us
where the time goes in v3:
time: 159 us
  Pallas kernels  155 us (97%)
  local copies, waits for them, and re-layouts  2.43 us (2%)
  other arithmetic  1.6 us (1%)
    pallas_call x1, Pallas kernels, local(): pl.pallas_call(functools.partial(kernel, nboson, nblock, row_tiles, col_b...  155 us

profile of v3, /device:TPU:17, one launch (start us, length us, event | category | flops | bytes accessed | tf_op | source)
XLA Modules:
  0.0 159.2 jit_solution(11712339950692048216)
XLA Ops:
  0.0 0.0 copy-start
  0.0 0.8 copy-done
  0.8 0.1 constant_dynamic-slice_fusion
  0.9 0.1 copy.8
  1.0 0.1 reshape.165
  1.1 0.2 convert_reduce_fusion
  1.3 0.0 copy-start.1
  1.3 0.7 select_reduce_fusion.2.back_slot
  2.0 0.7 select_reduce_fusion
  2.7 0.0 copy-done.1
  2.7 155.1 %window.1 = bf16[4,256,1024]{2,1,0:T(8,128)(2,1)S(1)} custom-call(s32[128]{0:T(128)} %copy-done.1, s32[136]{0:T(256)} %get-tuple-element.10.item_of, s32[128]{0:T(128)} %select_reduce_fusion.2.back_slot, s32[136]{0:T(256)} %get-tuple-element.9.back_item_of, bf16[4,256,1024]{2,1,0:T(8,128)(2,1)} %gamma_in.1, bf16[4,256,1024]{2,1,0:T(8,128)(2,1)} %full_in.1, ...), custom_call_target="tpu_custom_call" | custom-call | tf_op jit(solution)/shard_map/window/pallas_call | solution.py:296
  157.9 1.3 copy.10
  (2 shorter events, 0.0 us)
Async XLA Ops:
  0.0 0.8 copy-start
  1.3 1.4 copy-start.1

commit v4 on v3

--- a/solution.py
+++ b/solution.py
@@ -8,7 +8,8 @@
 
 MESH = pl.DeviceIdType.MESH
 DMA = pltpu.SemaphoreType.DMA
-PARTS = 4
+PARTS = 2
+LANES = 128
 
 
 def loop(start, stop, body):
@@ -161,11 +162,53 @@
     pl.semaphore_wait(barrier, len(block_peers) + len(boson_peers))
 
 
+def slot_tables(nboson, capacity, targets, rows):
+    row_tiles, col_blocks, _ = targets.shape
+    per_point = row_tiles * col_blocks
+    points = targets.shape[2] // nboson
+    total = points * per_point
+    boson = lax.axis_index("boson")
+    flat = targets[...].reshape(per_point, targets.shape[2])
+    lane = lax.broadcasted_iota(jnp.int32, flat.shape, 1)
+    own = jnp.concatenate(
+        [jnp.sum(jnp.where(lane == boson * points + q, flat, 0), axis=1, keepdims=True)
+         for q in range(points)], axis=0)
+    item = lax.broadcasted_iota(jnp.int32, (total, 1), 0)
+
+    def spread(keys, values, width):
+        wanted = lax.broadcasted_iota(jnp.int32, (total, width), 1)
+        return jnp.sum(jnp.where(keys == wanted, values, 0), axis=0, keepdims=True)
+
+    shift = ((own >> (points.bit_length() - 1)) - boson) & (nboson - 1)
+    target = (own & (points - 1)) * per_point + (item & (per_point - 1))
+    other = lax.broadcasted_iota(jnp.int32, (total, total), 1)
+    earlier = (spread(item, shift, total) == shift) & (other < item)
+    rank = jnp.sum(jnp.where(earlier, 1, 0), axis=1, keepdims=True)
+    send = ((boson + shift) & (nboson - 1)) * capacity + rank
+    recv = ((boson - shift) & (nboson - 1)) * capacity + rank
+    width = rows.shape[0] // 8 * rows.shape[1]
+    last_slot, last_item = nboson * capacity - 1, total - 1
+    for k, (keys, values, last) in enumerate((
+            (item, send, last_slot), (send, item, last_item),
+            (target, recv, last_slot), (recv, target, last_item))):
+        line = jnp.minimum(spread(keys, values, width), last)
+        for h in range(width // LANES):
+            rows[h * 8 + k:h * 8 + k + 1, :] = line[:, h * LANES:(h + 1) * LANES]
+
+
+class Table:
+    def __init__(self, ref, k):
+        self.ref, self.k = ref, k
+
+    def __getitem__(self, i):
+        return self.ref[i // LANES * 8 + self.k, i % LANES]
+
+
 def kernel(nboson, nblock, row_tiles, col_blocks,
-           send_slot, item_of, back_slot, back_item_of,
-           gamma_in, full_in, chi_ph, pp_in, chi_pp, out,
+           relabel, gamma_in, full_in, chi_ph, pp_in, chi_pp, out,
            full, pp, gamma, scaled, base, tiles, packed, landed, back, returned,
-           gamma_sem, ahead_s, ahead_r, home_s, home_r, *gather_sems):
+           targets, table_rows, table,
+           gamma_sem, table_sem, ahead_s, ahead_r, home_s, home_r, *gather_sems):
     half = len(gather_sems) // 2
     first = Gather(nblock, full_in, full, gather_sems[:half])
     second = Gather(nblock, pp_in, pp, gather_sems[half:])
@@ -174,10 +217,16 @@
     points, rows, order = gamma.shape
     high, wide = rows // row_tiles, order // col_blocks
     step = 2 * wide
+    capacity = landed.shape[1]
+    send_slot, item_of, back_slot, back_item_of = (Table(table, i) for i in range(4))
+    block_rows = pl.ds(lax.axis_index("block") * row_tiles, row_tiles)
+    load_targets = pltpu.make_async_copy(relabel.at[block_rows], targets, table_sem.at[0])
+    load_table = pltpu.make_async_copy(table_rows, table, table_sem.at[1])
     load_gamma = pltpu.make_async_copy(gamma_in, gamma, gamma_sem)
 
     first.own().start()
     load_gamma.start()
+    load_targets.start()
     second.own().start()
     greet(first.peers(), ahead.peers())
     first.start()
@@ -185,6 +234,9 @@
     load_gamma.wait()
     for q in range(points):
         scaled[q] = (gamma[q].astype(jnp.float32) * chi_ph[q:q + 1, :]).astype(jnp.bfloat16)
+    load_targets.wait()
+    slot_tables(nboson, capacity, targets, table_rows)
+    load_table.start()
     first.own().wait()
 
     def cut(wire, q, column):
@@ -215,6 +267,7 @@
     loop(1, first.chunks, one)
     first.sent_far()
     second.start()
+    load_table.wait()
     compute(first.chunks - 1)
     ahead.pack_and_start(tiles, item_of)
 
@@ -224,7 +277,6 @@
     loop(0, second.chunks, second.arrived)
     ahead.received()
 
-    capacity = landed.shape[1]
     flat = landed.reshape(nboson * capacity, high, wide)
     for p in range(points):
         for c in range(col_blocks):
@@ -255,31 +307,6 @@
     home.sent()
 
 
-def tables(relabel, points, row_tiles, nboson, capacity):
-    boson, block = lax.axis_index("boson"), lax.axis_index("block")
-    col_blocks = relabel.shape[2]
-    per_point = row_tiles * col_blocks
-    total = points * per_point
-    own = lax.dynamic_slice(
-        relabel, (boson * points, block * row_tiles, 0), (points, row_tiles, col_blocks)
-    ).reshape(total)
-    shifts = (own // points - boson) % nboson
-    items = jnp.arange(total, dtype=jnp.int32)
-    slots = jnp.arange(nboson * capacity, dtype=jnp.int32)
-    target = own % points * per_point + items % per_point
-    earlier = (shifts[None, :] == shifts[:, None]) & (items[None, :] < items[:, None])
-    rank = jnp.sum(earlier.astype(jnp.int32), axis=1)
-    send_slot = (boson + shifts) % nboson * capacity + rank
-    recv_slot = (boson - shifts) % nboson * capacity + rank
-
-    def pick(keys, wanted, values):
-        hit = (keys[None, :] == wanted[:, None]).astype(jnp.int32)
-        return jnp.sum(hit * values[None, :], axis=1)
-
-    return (send_slot, pick(send_slot, slots, items), pick(target, items, recv_slot),
-            pick(recv_slot, slots, target))
-
-
 def local(nboson, nblock, gamma_ph, full_ph, chi_ph, pp_vertex, chi_pp, relabel):
     points, rows, order = gamma_ph.shape
     row_tiles, col_blocks = relabel.shape[1] // nblock, relabel.shape[2]
@@ -290,22 +317,25 @@
     whole = pltpu.VMEM((points, order, order), bf16)
     shard = pltpu.VMEM(gamma_ph.shape, bf16)
     slabs = pltpu.VMEM((nboson, capacity, high, wide), bf16)
-    smem = pl.BlockSpec(memory_space=pltpu.SMEM)
+    table_rows = -(-(nboson * capacity) // LANES) * 8
+    for count in (nboson, points, row_tiles * col_blocks):
+        assert count & (count - 1) == 0
     vmem = pl.BlockSpec(memory_space=pltpu.VMEM)
     hbm = pl.BlockSpec(memory_space=pl.ANY)
     return pl.pallas_call(
         functools.partial(kernel, nboson, nblock, row_tiles, col_blocks),
         out_shape=pltpu.VMEM(gamma_ph.shape, bf16), name="window",
-        in_specs=[smem] * 4 + [hbm, hbm, vmem, hbm, vmem], out_specs=vmem,
+        in_specs=[hbm, hbm, hbm, vmem, hbm, vmem], out_specs=vmem,
         scratch_shapes=[
             whole, whole, shard, shard, pltpu.VMEM(gamma_ph.shape, f32),
             pltpu.VMEM((total, high, wide), bf16), slabs, slabs, slabs, slabs,
-            DMA, DMA((nboson,)), DMA((nboson,)), DMA((nboson,)), DMA((nboson,)),
+            pltpu.VMEM((row_tiles,) + (relabel.shape[2], relabel.shape[0]), jnp.int32),
+            pltpu.VMEM((table_rows, LANES), jnp.int32), pltpu.SMEM((table_rows, LANES), jnp.int32),
+            DMA, DMA((2,)), DMA((nboson,)), DMA((nboson,)), DMA((nboson,)), DMA((nboson,)),
         ] + gather_scratch(nblock, points) + gather_scratch(nblock, points),
         compiler_params=pltpu.CompilerParams(
             collective_id=0, has_side_effects=True, vmem_limit_bytes=60 * 1024 * 1024),
-    )(*tables(relabel, points, row_tiles, nboson, capacity),
-      gamma_ph, full_ph, chi_ph, pp_vertex, chi_pp)
+    )(relabel.transpose(1, 2, 0), gamma_ph, full_ph, chi_ph, pp_vertex, chi_pp)
 
 
 def solution(mesh):

time: 159 us -> 156 us (0.981)
  other arithmetic: 1.6 us -> 0 us
where the time goes in v4:
time: 156 us
  Pallas kernels  154 us (99%)
    pallas_call x1, Pallas kernels, local(): pl.pallas_call(functools.partial(kernel, nboson, nblock, row_tiles, col_b...  154 us

profile of v4, /device:TPU:17, one launch (start us, length us, event | category | flops | bytes accessed | tf_op | source)
XLA Modules:
  0.0 155.6 jit_solution(17388938063683599350)
XLA Ops:
  0.0 154.3 %window.1 = bf16[4,256,1024]{2,1,0:T(8,128)(2,1)S(1)} custom-call(s32[16,8,32]{2,1,0:T(8,128)} %bitcast.1, bf16[4,256,1024]{2,1,0:T(8,128)(2,1)} %gamma_in.1, bf16[4,256,1024]{2,1,0:T(8,128)(2,1)} %full_in.1, f32[4,1024]{1,0:T(4,128)} %chi_ph.1, bf16[4,256,1024]{2,1,0:T(8,128)(2,1)} %pp_in.1, f32[4,1024]{1,0:T(4,128)} %chi_pp.1), custom_call_target="tpu_custom_call" | custom-call | tf_op jit(solution)/shard_map/window/pallas_call | solution.py:325
  154.3 1.3 copy.8

commit v5 on v4

--- a/solution.py
+++ b/solution.py
@@ -120,7 +120,8 @@
         return [(self.boson + s) % self.n for s in range(1, self.n)]
 
     def shift(self, i):
-        return self.n // 2 + (1 - 2 * (i % 2)) * ((i + 1) // 2)
+        upper = self.boson // (self.n // 2)
+        return (i + 1) * (1 - upper) + (self.n - 1 - i) * upper
 
     def copy(self, s, slot):
         dest = (self.boson + s) % self.n

time: 156 us -> 158 us (1.013)
  the two profiles are of different devices: /device:TPU:17 before, /device:TPU:0 now
where the time goes in v5:
time: 158 us; the launch traced here: 157 us
  Pallas kernels  156 us (99%)
    pallas_call x1, Pallas kernels, local(): pl.pallas_call(functools.partial(kernel, nboson, nblock, row_tiles, col_b...  156 us

profile of v5, /device:TPU:0, one launch (start us, length us, event | category | flops | bytes accessed | tf_op | source)
XLA Modules:
  0.0 157.4 jit_solution(931973787316272475)
XLA Ops:
  0.0 156.1 %window.1 = bf16[4,256,1024]{2,1,0:T(8,128)(2,1)S(1)} custom-call(s32[16,8,32]{2,1,0:T(8,128)} %bitcast.1, bf16[4,256,1024]{2,1,0:T(8,128)(2,1)} %gamma_in.1, bf16[4,256,1024]{2,1,0:T(8,128)(2,1)} %full_in.1, f32[4,1024]{1,0:T(4,128)} %chi_ph.1, bf16[4,256,1024]{2,1,0:T(8,128)(2,1)} %pp_in.1, f32[4,1024]{1,0:T(4,128)} %chi_pp.1), custom_call_target="tpu_custom_call" | custom-call | tf_op jit(solution)/shard_map/window/pallas_call | solution.py:326
  156.1 1.3 copy.8
